TPU v7x, 32 devices: a whole 2x2x4 slice. The times are simulated.
32 devices in a mesh: fsdp: 8 (over y, x, core), tensor: 4 (over z).
Axes of the slice: x: 2, y: 2, z: 4, core: 2. Of those that a mesh axis runs over, the one named last changes fastest.
Arguments:
- tokens: bfloat16 [8192, 4096], P('fsdp'), may hold values from -6 to 6
- input_source: float32 [256, 16, 4096], P('tensor', None, 'fsdp'), may hold values from -0.09375 to 0.09375
- branch_source: float32 [256, 16, 4096], P('tensor', None, 'fsdp'), may hold values from -0.09375 to 0.09375
- output_source: float32 [256, 16, 4096], P('tensor', None, 'fsdp'), may hold values from -0.09375 to 0.09375
- gates_source: float32 [2, 16, 256, 256], P(None, None, 'fsdp', 'tensor'), may hold values from -0.375 to 0.375
- decay_param: float32 [16, 256], replicated, may hold values from -9 to 1
- block_order: int32 [16], replicated, may hold values from 0 to 15, each once
Outputs:
- mixed: bfloat16 [8192, 4096], P('fsdp', 'tensor')
- input_serve: bfloat16 [4096, 4096], P(None, 'tensor')
- branch_serve: bfloat16 [4096, 4096], P(None, 'tensor')
- output_serve: bfloat16 [4096, 4096], P(None, 'tensor')
- gates_serve: bfloat16 [2, 16, 256, 256], P(None, 'tensor')
Inputs may be any that keep to these rules, and one draw needn't show every extreme that they name: `block_order`: every gate block appears exactly once.
All inputs are finite; a program needn't handle non-finite values.
Results may differ from a plain program's by a relative error of at most 0.013.
Values may be sent and summed in bfloat16 or wider, within the bound.
A program may use at most 128 MiB of HBM per device.

v0:
```python
import functools
import jax
import jax.numpy as jnp
from jax import lax
from jax.experimental import pallas as pl
from jax.experimental.pallas import tpu as pltpu
from jax.sharding import PartitionSpec as P

LEN = 256
SUB = 8


def for_sending(shard):
    return jax.tree.map(lambda a: a.astype(jnp.bfloat16) if a.dtype == jnp.float32 else a, shard)


def recur_body(prompts, x_ref, pre_ref, g_ref, r_ref, o_ref, a_s, d_s, carry):
    @pl.when(pl.program_id(1) == 0)
    def _():
        carry[...] = jnp.zeros_like(carry)

    dims = (((1,), (1,)), ((), ()))
    x = x_ref[...]
    pre_r = lax.dot_general(x, g_ref[0, 0], dims, preferred_element_type=jnp.float32)
    pre_i = lax.dot_general(x, g_ref[1, 0], dims, preferred_element_type=jnp.float32)
    a = jnp.exp(r_ref[0] * jax.nn.sigmoid(pre_r))
    a_s[...] = a
    d_s[...] = jnp.sqrt(jnp.maximum(1.0 - a * a, 0.0)) * (
        jax.nn.sigmoid(pre_i) * x.astype(jnp.float32)
    )
    rows, chan = a_s.shape
    group = lax.broadcasted_iota(jnp.int32, (SUB, chan), 0) // prompts

    def last(v):
        res = v
        for g in range(SUB // prompts - 1):
            res = jnp.where(group == g, pltpu.roll(v, (g + 1) * prompts, 0), res)
        return res

    def step(i, c):
        at = pl.ds(pl.multiple_of(i * SUB, SUB), SUB)
        a = a_s[at, :]
        d = d_s[at, :]
        shift = 1
        while shift < SUB // prompts:
            a_sh = pltpu.roll(a, shift * prompts, 0)
            d_sh = pltpu.roll(d, shift * prompts, 0)
            d = jnp.where(group >= shift, a * d_sh + d, d)
            a = jnp.where(group >= shift, a * a_sh, a)
            shift *= 2
        d_s[at, :] = a * c + d
        return last(a) * c + last(d)

    carry[...] = lax.fori_loop(0, rows // SUB, step, carry[...], unroll=8)
    o_ref[...] = (d_s[...] * jax.nn.gelu(pre_ref[...], approximate=True)).astype(o_ref.dtype)


def recur(branch_in, gate_pre, gates, rate, prompts):
    rows, width = branch_in.shape
    blocks, chan = gates.shape[1], gates.shape[2]
    tile = min(rows, 256)
    return pl.pallas_call(
        functools.partial(recur_body, prompts),
        grid=(blocks, rows // tile),
        in_specs=[
            pl.BlockSpec((tile, chan), lambda b, t: (t, b)),
            pl.BlockSpec((tile, chan), lambda b, t: (t, b)),
            pl.BlockSpec((2, 1, chan, chan), lambda b, t: (0, b, 0, 0)),
            pl.BlockSpec((1, 1, chan), lambda b, t: (b, 0, 0)),
        ],
        out_specs=pl.BlockSpec((tile, chan), lambda b, t: (t, b)),
        out_shape=jax.ShapeDtypeStruct((rows, width), jnp.bfloat16),
        scratch_shapes=[
            pltpu.VMEM((tile, chan), jnp.float32),
            pltpu.VMEM((tile, chan), jnp.float32),
            pltpu.VMEM((SUB, chan), jnp.float32),
        ],
        compiler_params=pltpu.CompilerParams(dimension_semantics=("arbitrary", "arbitrary")),
        cost_estimate=pl.CostEstimate(
            flops=4 * rows * width * chan, bytes_accessed=8 * rows * width, transcendentals=6 * rows * width
        ),
        name="recur",
    )(branch_in, gate_pre, gates, rate)


def on_device(
    tokens, input_source, branch_source, output_source, gates_source, decay_param, block_order
):
    tensor_count = lax.axis_size("tensor")
    per_dev = block_order.shape[0] // tensor_count
    own_blocks = lax.dynamic_slice_in_dim(block_order, lax.axis_index("tensor") * per_dev, per_dev)
    casted = (
        input_source.astype(jnp.bfloat16),
        branch_source.astype(jnp.bfloat16),
        output_source.astype(jnp.bfloat16),
    )
    gate_cast = gates_source.astype(jnp.bfloat16)
    sectioned = tuple((jnp.take(weight, block_order, axis=1) for weight in casted))
    regrouped = jax.tree.map(
        lambda part, own: part.astype(own.dtype),
        lax.all_to_all(for_sending(sectioned), "tensor", split_axis=1, concat_axis=0, tiled=True),
        sectioned,
    )
    gate_sectioned = jnp.take(gate_cast, block_order, axis=1)
    gate_group = lax.all_to_all(gate_sectioned, "tensor", split_axis=1, concat_axis=3, tiled=True)
    pieces = tuple(
        (jnp.transpose(weight, (2, 1, 0)).reshape(weight.shape[2], -1) for weight in regrouped)
    )
    gate_piece = jnp.transpose(gate_group, (0, 1, 3, 2))
    gates_serve = lax.all_gather(gate_piece, "fsdp", axis=3, tiled=True)
    row_count = tokens.shape[0]
    input_serve = lax.all_gather(pieces[0], "fsdp", axis=0, tiled=True)
    branch_serve = lax.all_gather(pieces[1], "fsdp", axis=0, tiled=True)
    output_serve = lax.all_gather(pieces[2], "fsdp", axis=0, tiled=True)
    rate = -8.0 * jax.nn.softplus(jnp.take(decay_param, own_blocks, axis=0))[:, None, :]
    branch_in = jnp.dot(tokens, input_serve, preferred_element_type=jnp.float32).astype(jnp.bfloat16)
    gate_pre = jnp.dot(tokens, branch_serve, preferred_element_type=jnp.float32)
    gated = recur(branch_in, gate_pre, gates_serve, rate, row_count // LEN)
    parts = []
    for rows in jnp.split(gated, 2, axis=0):
        partial_value = lax.dot_general(
            rows, output_serve, (((1,), (1,)), ((), ())), preferred_element_type=jnp.float32
        )
        parts.append(
            lax.psum_scatter(
                partial_value.astype(jnp.bfloat16), "tensor", scatter_dimension=1, tiled=True
            )
        )
    mixed = jnp.concatenate(parts, axis=0)
    return (mixed, input_serve, branch_serve, output_serve, gates_serve)


def solution(mesh):
    return jax.shard_map(
        on_device,
        mesh=mesh,
        in_specs=(
            P("fsdp", None),
            P("tensor", None, "fsdp"),
            P("tensor", None, "fsdp"),
            P("tensor", None, "fsdp"),
            P(None, None, "fsdp", "tensor"),
            P(),
            P(),
        ),
        out_specs=(
            P("fsdp", "tensor"),
            P(None, "tensor"),
            P(None, "tensor"),
            P(None, "tensor"),
            P(None, "tensor", None, None),
        ),
        check_vma=False,
    )
```

profile of v0, /device:TPU:0, one launch (start us, length us, event | category | flops | bytes accessed | tf_op | source)
XLA Modules:
  0.0 434.1 jit_solution(17604872154267987698)
XLA Ops:
  7.2 0.0 copy-start
  7.2 0.7 compare_select_fusion.1
  7.8 0.7 compare_and_fusion
  8.5 0.0 copy-start.3
  8.5 1.1 convert_element_type.27
  9.6 0.6 gather_fusion
  10.2 0.1 fusion.3
  10.3 0.9 reshape.140
  11.2 6.3 %all-to-all-start.2 = ((bf16[4,2,8192]{2,1,0:T(2,128)(2,1)}), bf16[4,2,8192]{2,1,0:T(2,128)(2,1)S(1)}, u32[]{:S(2)}, u32[]{:S(2)}) async-start(bf16[4,2,8192]{2,1,0:T(2,128)(2,1)} %reshape.140), calls=%async_computation.2 | async-start | bytes 262144 | tf_op jit(solution)/shard_map/all_to_all | solution.py:105
  17.6 0.0 all-gather.9.cloned.1.call-start
  17.6 0.0 copy-done.3
  17.6 2.7 copy.52
  20.3 0.6 gather_fusion.2
  20.9 2.7 copy.51
  23.6 0.6 gather_fusion.3
  24.2 3.7 copy.50
  27.9 1.8 gather_fusion.4
  29.8 0.0 all-to-all-done.2
  29.8 0.2 reshape.141
  30.0 0.9 copy.53
  30.9 1.8 all_to_all.63
  32.7 0.0 all-gather.9.cloned.1.call-update
  32.8 0.0 all-gather.7.cloned.1.call-start
  32.8 2.3 select_bitcast_fusion.1
  35.1 30.2 %all_to_all.72 = bf16[64,16,512]{2,0,1:T(8,128)(2,1)S(1)} all-to-all(bf16[64,16,512]{2,0,1:T(8,128)(2,1)S(1)} %get-tuple-element.13), channel_id=1, replica_groups=mesh['fsdp'=8,'tensor'=4] {'tensor'}, dimensions={1} | all-to-all | bytes 2097152 | tf_op jit(solution)/shard_map/all_to_all | solution.py:101
  65.3 0.1 copy.35
  65.4 1.3 copy.36
  66.7 0.0 all-gather.7.cloned.1.call-update
  66.7 0.0 all-gather.5.cloned.1.call-start
  66.8 28.2 %all_to_all.73 = bf16[64,16,512]{2,0,1:T(8,128)(2,1)S(1)} all-to-all(bf16[64,16,512]{2,0,1:T(8,128)(2,1)} %get-tuple-element.15), channel_id=1, replica_groups=mesh['fsdp'=8,'tensor'=4] {'tensor'}, dimensions={1} | all-to-all | bytes 2097152 | tf_op jit(solution)/shard_map/all_to_all | solution.py:101
  95.0 0.1 copy.31
  95.1 1.3 copy.32
  96.4 0.0 all-gather.5.cloned.1.call-update
  96.5 0.0 all-gather.11.cloned.1.call-start
  96.5 0.0 copy-done.2
  96.5 27.5 %all_to_all.74 = bf16[64,16,512]{2,0,1:T(8,128)(2,1)S(1)} all-to-all(bf16[64,16,512]{2,0,1:T(8,128)(2,1)S(1)} %copy-done.2), channel_id=1, replica_groups=mesh['fsdp'=8,'tensor'=4] {'tensor'}, dimensions={1} | all-to-all | bytes 2097152 | tf_op jit(solution)/shard_map/all_to_all | solution.py:101
  124.1 0.1 copy.41
  124.1 1.3 copy.42
  125.5 0.0 all-gather.11.cloned.1.call-update
  125.5 0.2 reduce-scatter.3.cloned.1.call-start
  125.7 0.0 copy-done.4
  125.7 0.1 compare_and_fusion.1
  125.8 0.0 copy-done
  125.8 0.6 gather_fusion.1
  126.4 0.7 fusion.2.r_ref
  127.1 2.4 copy.39.g_ref
  129.5 15.6 %convolution_bitcast_fusion.pre_ref = f32[1024,1024]{1,0:T(8,128)} fusion(bf16[1024,4096]{1,0:T(8,128)(2,1)} %param.9, bf16[4096,1024]{1,0:T(8,128)(2,1)} %all-gather.7.cloned.1.call-done), kind=kOutput, calls=%fused_computation.7 | convolution fusion | flops 8589934592 | bytes 20971520 | tf_op jit(solution)/shard_map/dot_general | solution.py:117
  145.1 31.9 %all-gather.5.cloned.1.call-done = bf16[4096,1024]{1,0:T(8,128)(2,1)} async-done(((bf16[512,1024]{1,0:T(8,128)(2,1)}), bf16[4096,1024]{1,0:T(8,128)(2,1)}) %all-gather.5.cloned.1.call-update) | async-done | bytes 8388624 | tf_op jit(solution)/shard_map/all_gather | solution.py:112
  177.0 14.6 %convert_bitcast_fusion.x_ref = bf16[1024,1024]{1,0:T(8,128)(2,1)} fusion(bf16[1024,4096]{1,0:T(8,128)(2,1)} %param.9, bf16[4096,1024]{1,0:T(8,128)(2,1)} %all-gather.5.cloned.1.call-done), kind=kOutput, calls=%fused_computation.12 | convolution fusion | flops 8590983168 | bytes 18874368 | tf_op jit(solution)/shard_map/dot_general | solution.py:116
  191.6 16.2 %recur.1 = bf16[1024,1024]{1,0:T(8,128)(2,1)} custom-call(bf16[1024,1024]{1,0:T(8,128)(2,1)} %convert_bitcast_fusion.x_ref, f32[1024,1024]{1,0:T(8,128)} %convolution_bitcast_fusion.pre_ref, bf16[2,4,256,256]{3,2,1,0:T(8,128)(2,1)} %copy.39.g_ref, f32[4,1,256]{2,1,0:T(1,128)} %fusion.2.r_ref), custom_call_target="tpu_custom_call" | custom-call | flops 1073741824 | bytes 8388608 | tf_op jit(solution)/shard_map/recur/pallas_call | solution.py:62
  207.9 25.8 %all-gather.11.cloned.1.call-done = bf16[4096,1024]{1,0:T(8,128)(2,1)} async-done(((bf16[512,1024]{1,0:T(8,128)(2,1)}), bf16[4096,1024]{1,0:T(8,128)(2,1)}) %all-gather.11.cloned.1.call-update) | async-done | bytes 8388624 | tf_op jit(solution)/shard_map/all_gather | solution.py:114
  233.6 10.3 %convolution_convert_fusion.1 = bf16[512,4096]{1,0:T(8,128)(2,1)} fusion(bf16[4096,1024]{1,0:T(8,128)(2,1)} %all-gather.11.cloned.1.call-done, bf16[1024,1024]{1,0:T(8,128)(2,1)} %recur.1), kind=kOutput, calls=%fused_computation.6 | convolution fusion | flops 4297064448 | bytes 13631488 | tf_op jit(solution)/shard_map/dot_general | solution.py:121
  243.9 0.0 reduce-scatter.3.cloned.1.call-update
  243.9 0.3 reduce-scatter.5.cloned.1.call-start
  244.2 0.0 copy-done.5
  244.2 9.5 %convolution_convert_fusion = bf16[512,4096]{1,0:T(8,128)(2,1)} fusion(bf16[4096,1024]{1,0:T(8,128)(2,1)} %all-gather.11.cloned.1.call-done, bf16[1024,1024]{1,0:T(8,128)(2,1)S(1)} %copy-done.5), kind=kOutput, calls=%fused_computation.5 | convolution fusion | flops 4297064448 | bytes 13631488 | tf_op jit(solution)/shard_map/dot_general | solution.py:121
  253.7 0.0 reduce-scatter.5.cloned.1.call-update
  253.7 67.1 %reduce-scatter.3.cloned.1.call-done = bf16[512,1024]{1,0:T(8,128)(2,1)} async-done(((bf16[512,4096]{1,0:T(8,128)(2,1)}), bf16[512,1024]{1,0:T(8,128)(2,1)}) %reduce-scatter.3.cloned.1.call-update) | async-done | bytes 1048592 | tf_op jit(solution)/shard_map/reduce_scatter | solution.py:125
  320.9 80.1 %reduce-scatter.5.cloned.1.call-done = bf16[512,1024]{1,0:T(8,128)(2,1)} async-done(((bf16[512,4096]{1,0:T(8,128)(2,1)}), bf16[512,1024]{1,0:T(8,128)(2,1)}) %reduce-scatter.5.cloned.1.call-update) | async-done | bytes 1048592 | tf_op jit(solution)/shard_map/reduce_scatter | solution.py:125
  400.9 3.0 pad_maximum_fusion
  403.9 7.8 %copy.57 = bf16[4096,1024]{1,0:T(8,128)(2,1)} copy(bf16[4096,1024]{1,0:T(8,128)(2,1)} %all-gather.5.cloned.1.call-done) | data formatting | bytes 16777216
  411.7 7.8 %copy.58 = bf16[4096,1024]{1,0:T(8,128)(2,1)} copy(bf16[4096,1024]{1,0:T(8,128)(2,1)} %all-gather.7.cloned.1.call-done) | data formatting | bytes 16777216
  419.5 7.8 %copy.59 = bf16[4096,1024]{1,0:T(8,128)(2,1)} copy(bf16[4096,1024]{1,0:T(8,128)(2,1)} %all-gather.11.cloned.1.call-done) | data formatting | bytes 16777216
  427.2 0.0 copy-done.1
  (8 shorter events, 0.0 us)
Async XLA Ops:
  7.2 118.7 %copy-start = (f32[16,256]{1,0:T(8,128)S(1)}, f32[16,256]{1,0:T(8,128)}, u32[]{:S(2)}) copy-start(f32[16,256]{1,0:T(8,128)} %param.14) | copy-start | bytes 49156
  8.5 9.1 %copy-start.3 = (pred[16]{0:T(512)(128)(4,1)}, pred[16]{0:T(512)(128)(4,1)S(1)}, u32[]{:S(2)}) copy-start(pred[16]{0:T(512)(128)(4,1)S(1)} %compare_and_fusion) | copy-start | bytes 52
  11.2 18.5 %all-to-all-start.2 = ((bf16[4,2,8192]{2,1,0:T(2,128)(2,1)}), bf16[4,2,8192]{2,1,0:T(2,128)(2,1)S(1)}, u32[]{:S(2)}, u32[]{:S(2)}) async-start(bf16[4,2,8192]{2,1,0:T(2,128)(2,1)} %reshape.140), calls=%async_computation.2 | async-start | bytes 262144 | tf_op jit(solution)/shard_map/all_to_all | solution.py:105
  17.6 109.5 %all-gather.9.cloned.1.call-start = ((), (), s32[]{:S(2)}) async-start(), calls=%async_computation.8 | async-start | bytes 1179648 | tf_op jit(solution)/shard_map/all_gather | solution.py:110
  32.8 96.7 %all-gather.7.cloned.1.call-start = ((), (), s32[]{:S(2)}) async-start(), calls=%async_computation.7 | async-start | bytes 9437184 | tf_op jit(solution)/shard_map/all_gather | solution.py:113
  35.1 61.4 %copy-start.2 = (bf16[64,16,512]{2,0,1:T(8,128)(2,1)S(1)}, bf16[64,16,512]{2,0,1:T(8,128)(2,1)}, u32[]{:S(2)}) copy-start(bf16[64,16,512]{2,0,1:T(8,128)(2,1)} %get-tuple-element.14) | copy-start | bytes 3145732
  66.7 59.0 %copy-start.4 = (s32[16]{0:T(128)S(1)}, s32[16]{0:T(128)}, u32[]{:S(2)}) copy-start(s32[16]{0:T(128)} %param.15) | copy-start | bytes 196
  66.7 110.3 %all-gather.5.cloned.1.call-start = ((), (), s32[]{:S(2)}) async-start(), calls=%async_computation.6 | async-start | bytes 9437184 | tf_op jit(solution)/shard_map/all_gather | solution.py:112
  96.5 137.2 %all-gather.11.cloned.1.call-start = ((), (), s32[]{:S(2)}) async-start(), calls=%async_computation.9 | async-start | bytes 9437184 | tf_op jit(solution)/shard_map/all_gather | solution.py:114
  125.5 195.4 %reduce-scatter.3.cloned.1.call-start = ((), (), s32[]{:S(2)}) async-start(), calls=%async_computation.10 | async-start | bytes 5242880 | tf_op jit(solution)/shard_map/reduce_scatter | solution.py:125
  207.9 36.4 %copy-start.5 = (bf16[1024,1024]{1,0:T(8,128)(2,1)S(1)}, bf16[1024,1024]{1,0:T(8,128)(2,1)}, u32[]{:S(2)}) copy-start(bf16[1024,1024]{1,0:T(8,128)(2,1)} %recur.1) | copy-start | bytes 6291460
  243.9 157.0 %reduce-scatter.5.cloned.1.call-start = ((), (), s32[]{:S(2)}) async-start(), calls=%async_computation.11 | async-start | bytes 5242880 | tf_op jit(solution)/shard_map/reduce_scatter | solution.py:125
  411.7 15.5 %copy-start.1 = (f32[16,256]{1,0:T(8,128)S(1)}, f32[16,256]{1,0:T(8,128)}, u32[]{:S(2)}) copy-start(f32[16,256]{1,0:T(8,128)} %param.14) | copy-start | bytes 49156
Sparse Core Ops, SparseCore 0:
  32.9 24.8 all-gather.8
  66.9 53.3 all-gather.6
  122.7 54.2 all-gather.4
  179.3 54.2 all-gather.10
  244.1 76.7 reduce-scatter.2
  323.6 77.2 reduce-scatter.4
where the time goes:
time: 435 us; the launch traced here: 434 us
  waiting for transfers between devices  205 us (47%)
  blocking collectives  86 us (20%)
  matrix products  50 us (11%)
  local copies, waits for them, and re-layouts  47.1 us (11%)
  Pallas kernels  16.2 us (4%)
  between operations  14.2 us (3%)
  other arithmetic  8.62 us (2%)
  starting transfers between devices  6.96 us (2%)
    reduce_scatter x2, waiting for transfers between devices, on_device(): lax.psum_scatter(partial_value.astype(jnp.bfloat16), 'tensor', scatter_di...  147 us
    all_to_all x3, blocking collectives, on_device(): lax.all_to_all(for_sending(sectioned), 'tensor', split_axis=1, concat_axi...  86 us
    unnamed x20, local copies, waits for them, and re-layouts  33.5 us
    all_gather x1, waiting for transfers between devices, on_device(): input_serve = lax.all_gather(pieces[0], 'fsdp', axis=0, tiled=True)  31.9 us
    all_gather x1, waiting for transfers between devices, on_device(): output_serve = lax.all_gather(pieces[2], 'fsdp', axis=0, tiled=True)  25.8 us
    dot_general x2, matrix products, on_device(): lax.dot_general(rows, output_serve, (((1,), (1,)), ((), ())), preferred_e...  19.7 us
    pallas_call x1, Pallas kernels, recur(): pl.pallas_call(functools.partial(recur_body, prompts), grid=(blocks, rows...  16.2 us
    dot_general x1, matrix products, on_device(): gate_pre = jnp.dot(tokens, branch_serve, preferred_element_type=jnp.float32)  15.6 us
  transfers between devices with their start and end apart: 7, of which 4 were waited for; matrix products, arithmetic and copies ran while one was open for 14% of the time, Pallas kernels for 4%

commit v1 on v0

--- a/solution.py
+++ b/solution.py
@@ -8,10 +8,7 @@
 
 LEN = 256
 SUB = 8
-
-
-def for_sending(shard):
-    return jax.tree.map(lambda a: a.astype(jnp.bfloat16) if a.dtype == jnp.float32 else a, shard)
+MESH = pl.DeviceIdType.MESH
 
 
 def recur_body(prompts, x_ref, pre_ref, g_ref, r_ref, o_ref, a_s, d_s, carry):
@@ -83,6 +80,146 @@
     )(branch_in, gate_pre, gates, rate)
 
 
+def spread_body(g0, g1, g2, out0, out1, piece2, held, piece, own_sem, z_send, z_recv, put_sem, f_send, f_recv):
+    gs, outs = (g0, g1, g2), (out0, out1)
+    z, f = lax.axis_index("tensor"), lax.axis_index("fsdp")
+    zs = held.shape[1]
+    per = held.shape[2]
+    rows = piece.shape[1]
+    half = rows // 2
+    sib = f + 1 - 2 * (f % 2)
+    xp = f + 2 - 4 * ((f // 2) % 2)
+    yp = f + 4 - 8 * (f // 4)
+
+    barrier = pltpu.get_barrier_semaphore()
+    for peer in (sib, xp, yp):
+        pl.semaphore_signal(barrier, inc=1, device_id={"fsdp": peer}, device_id_type=MESH)
+    for k in range(1, zs):
+        pl.semaphore_signal(
+            barrier, inc=1, device_id={"tensor": (z + k) % zs}, device_id_type=MESH
+        )
+    pl.semaphore_wait(barrier, 3 + zs - 1)
+
+    a2a, own = {}, {}
+    for w in range(3):
+        for k in range(1, zs):
+            to = (z + k) % zs
+            a2a[w, k] = pltpu.make_async_remote_copy(
+                src_ref=gs[w].at[pl.ds(to * per, per)],
+                dst_ref=held.at[w, z],
+                send_sem=z_send.at[w, k],
+                recv_sem=z_recv.at[w, k],
+                device_id={"tensor": to},
+                device_id_type=MESH,
+            )
+            a2a[w, k].start()
+        own[w] = pltpu.make_async_copy(gs[w].at[pl.ds(z * per, per)], held.at[w, z], own_sem.at[w])
+        own[w].start()
+
+    def assemble(w, dst):
+        own[w].wait()
+        for k in range(1, zs):
+            a2a[w, k].wait_recv()
+        for b in range(per):
+            slab = jnp.concatenate([held[w, s, b] for s in range(zs)], axis=0)
+            width = slab.shape[0]
+            dst[:, b * width : (b + 1) * width] = slab.T
+
+    sent = {}
+
+    def send(w, i, src, start, count, peer):
+        at = outs[w].at[pl.ds(start, count)]
+        sent[w, i] = pltpu.make_async_remote_copy(
+            src_ref=at if src is None else src,
+            dst_ref=at,
+            send_sem=f_send.at[w, i],
+            recv_sem=f_recv.at[w, i],
+            device_id={"fsdp": peer},
+            device_id_type=MESH,
+        )
+        sent[w, i].start()
+
+    put = {}
+    diag = xp + 4 - 8 * (xp // 4)
+    for w in range(2):
+        assemble(w, piece.at[w])
+        send(w, 0, piece.at[w], f * rows, rows, xp)
+        send(w, 1, piece.at[w], f * rows, rows, yp)
+        send(w, 2, piece.at[w], f * rows, rows, sib)
+        put[w] = pltpu.make_async_copy(piece.at[w], outs[w].at[pl.ds(f * rows, rows)], put_sem.at[w])
+        put[w].start()
+    for w in range(2):
+        sent[w, 0].wait_recv()
+        send(w, 3, None, xp * rows, half, yp)
+        send(w, 4, None, xp * rows, rows, sib)
+        sent[w, 1].wait_recv()
+        send(w, 5, None, yp * rows + half, half, xp)
+        send(w, 6, None, yp * rows, rows, sib)
+        if w == 0:
+            assemble(2, piece2)
+    for w in range(2):
+        sent[w, 3].wait_recv()
+        send(w, 7, None, diag * rows, half, sib)
+        sent[w, 5].wait_recv()
+        send(w, 8, None, diag * rows + half, half, sib)
+    for w in range(2):
+        for i in (2, 4, 6, 7, 8):
+            sent[w, i].wait_recv()
+        for i in range(9):
+            sent[w, i].wait_send()
+        put[w].wait()
+    for w in range(3):
+        for k in range(1, zs):
+            a2a[w, k].wait_send()
+
+
+def spread(groups, zs, fs):
+    blocks, chan, rows = groups[0].shape
+    per = blocks // zs
+    width = per * chan * zs
+    full = jax.ShapeDtypeStruct((rows * fs, width), jnp.bfloat16)
+    vmem = pl.BlockSpec(memory_space=pltpu.VMEM)
+    hbm = pl.BlockSpec(memory_space=pl.ANY)
+    dma = pltpu.SemaphoreType.DMA
+    return pl.pallas_call(
+        spread_body,
+        in_specs=[vmem] * 3,
+        out_specs=[hbm, hbm, vmem],
+        out_shape=[full, full, jax.ShapeDtypeStruct((rows, width), jnp.bfloat16)],
+        scratch_shapes=[
+            pltpu.VMEM((3, zs, per, chan, rows), jnp.bfloat16),
+            pltpu.VMEM((2, rows, width), jnp.bfloat16),
+            dma((3,)),
+            dma((3, zs)),
+            dma((3, zs)),
+            dma((2,)),
+            dma((2, 9)),
+            dma((2, 9)),
+        ],
+        compiler_params=pltpu.CompilerParams(collective_id=0, has_side_effects=True),
+        name="spread",
+    )(*groups)
+
+
+def dup_body(x_ref, o_ref):
+    o_ref[...] = x_ref[...]
+
+
+def dup(x):
+    rows, width = x.shape
+    tile = min(rows, 512)
+    spec = pl.BlockSpec((tile, width), lambda i: (i, 0))
+    return pl.pallas_call(
+        dup_body,
+        grid=(rows // tile,),
+        in_specs=[spec],
+        out_specs=spec,
+        out_shape=jax.ShapeDtypeStruct(x.shape, x.dtype),
+        cost_estimate=pl.CostEstimate(flops=0, bytes_accessed=4 * rows * width, transcendentals=0),
+        name="dup",
+    )(x)
+
+
 def on_device(
     tokens, input_source, branch_source, output_source, gates_source, decay_param, block_order
 ):
@@ -96,22 +233,23 @@
     )
     gate_cast = gates_source.astype(jnp.bfloat16)
     sectioned = tuple((jnp.take(weight, block_order, axis=1) for weight in casted))
-    regrouped = jax.tree.map(
-        lambda part, own: part.astype(own.dtype),
-        lax.all_to_all(for_sending(sectioned), "tensor", split_axis=1, concat_axis=0, tiled=True),
-        sectioned,
-    )
     gate_sectioned = jnp.take(gate_cast, block_order, axis=1)
     gate_group = lax.all_to_all(gate_sectioned, "tensor", split_axis=1, concat_axis=3, tiled=True)
-    pieces = tuple(
-        (jnp.transpose(weight, (2, 1, 0)).reshape(weight.shape[2], -1) for weight in regrouped)
-    )
     gate_piece = jnp.transpose(gate_group, (0, 1, 3, 2))
     gates_serve = lax.all_gather(gate_piece, "fsdp", axis=3, tiled=True)
     row_count = tokens.shape[0]
-    input_serve = lax.all_gather(pieces[0], "fsdp", axis=0, tiled=True)
-    branch_serve = lax.all_gather(pieces[1], "fsdp", axis=0, tiled=True)
-    output_serve = lax.all_gather(pieces[2], "fsdp", axis=0, tiled=True)
+    if lax.axis_size("fsdp") == 8:
+        groups = [jnp.transpose(weight, (1, 0, 2)) for weight in sectioned]
+        input_serve, branch_serve, output_piece = spread(groups, tensor_count, 8)
+    else:
+        regrouped = lax.all_to_all(sectioned, "tensor", split_axis=1, concat_axis=0, tiled=True)
+        pieces = tuple(
+            (jnp.transpose(weight, (2, 1, 0)).reshape(weight.shape[2], -1) for weight in regrouped)
+        )
+        input_serve = lax.all_gather(pieces[0], "fsdp", axis=0, tiled=True)
+        branch_serve = lax.all_gather(pieces[1], "fsdp", axis=0, tiled=True)
+        output_piece = pieces[2]
+    output_serve = lax.all_gather(output_piece, "fsdp", axis=0, tiled=True)
     rate = -8.0 * jax.nn.softplus(jnp.take(decay_param, own_blocks, axis=0))[:, None, :]
     branch_in = jnp.dot(tokens, input_serve, preferred_element_type=jnp.float32).astype(jnp.bfloat16)
     gate_pre = jnp.dot(tokens, branch_serve, preferred_element_type=jnp.float32)
@@ -127,7 +265,7 @@
             )
         )
     mixed = jnp.concatenate(parts, axis=0)
-    return (mixed, input_serve, branch_serve, output_serve, gates_serve)
+    return (mixed, dup(input_serve), dup(branch_serve), dup(output_serve), gates_serve)
 
 
 def solution(mesh):

time: 435 us -> 381 us (0.88)
  Pallas kernels: 16.2 us -> 149 us
  waiting for transfers between devices: 205 us -> 131 us
  blocking collectives: 86 us -> 12.2 us
  local copies, waits for them, and re-layouts: 47.1 us -> 17.3 us
  starting transfers between devices: 6.96 us -> 0.57 us
    pallas_call x0 -> x4, Pallas kernels: none -> 133 us  [the longest x1 106 us: spread(): pl.pallas_call(spread_body, in_specs=[vmem] * 3, out_specs=[hbm, hbm, vme...]
    all_to_all x3 -> x1, blocking collectives: 86 us -> 12.2 us  [on_device(): lax.all_to_all(gate_sectioned, 'tensor', split_axis=1, concat_axis=3, til...]
    all_gather x3 -> x1, waiting for transfers between devices: 57.6 us -> 11.5 us  [on_device(): output_serve = lax.all_gather(output_piece, 'fsdp', axis=0, tiled=True)]
    reduce_scatter x2, waiting for transfers between devices: 147 us -> 120 us  [on_device(): lax.psum_scatter(partial_value.astype(jnp.bfloat16), 'tensor', scatter_di...]
    unnamed x20 -> x15, local copies, waits for them, and re-layouts: 33.5 us -> 9.6 us
    all_to_all x1 -> x0, starting transfers between devices: 6.35 us -> none  [on_device(): lax.all_to_all(gate_sectioned, 'tensor', split_axis=1, concat_axis=3, til...]
  transfers between devices with their start and end apart: 7 -> 4, of which waited for: 4 -> 3; matrix products, arithmetic and copies ran while one was open for 14% -> 14% of each run, Pallas kernels for 4% -> 39%
where the time goes in v1:
time: 381 us; the launch traced here: 380 us
  Pallas kernels  149 us (39%)
  waiting for transfers between devices  131 us (34%)
  matrix products  47.1 us (12%)
  local copies, waits for them, and re-layouts  17.3 us (5%)
  between operations  13.9 us (4%)
  blocking collectives  12.2 us (3%)
  other arithmetic  8.13 us (2%)
    reduce_scatter x2, waiting for transfers between devices, on_device(): lax.psum_scatter(partial_value.astype(jnp.bfloat16), 'tensor', scatter_di...  120 us
    pallas_call x1, Pallas kernels, spread(): pl.pallas_call(spread_body, in_specs=[vmem] * 3, out_specs=[hbm, hbm, vme...  106 us
    pallas_call x3, Pallas kernels, dup(): pl.pallas_call(dup_body, grid=(rows // tile,), in_specs=[spec], out_specs...  26.9 us
    dot_general x2, matrix products, on_device(): lax.dot_general(rows, output_serve, (((1,), (1,)), ((), ())), preferred_e...  19.7 us
    pallas_call x1, Pallas kernels, recur(): pl.pallas_call(functools.partial(recur_body, prompts), grid=(blocks, rows...  16.2 us
    dot_general x1, matrix products, on_device(): gate_pre = jnp.dot(tokens, branch_serve, preferred_element_type=jnp.float32)  15.1 us
    dot_general x1, matrix products, on_device(): jnp.dot(tokens, input_serve, preferred_element_type=jnp.float32)  12.4 us
    all_to_all x1, blocking collectives, on_device(): lax.all_to_all(gate_sectioned, 'tensor', split_axis=1, concat_axis=3, til...  12.2 us
  transfers between devices with their start and end apart: 4, of which 3 were waited for; matrix products, arithmetic and copies ran while one was open for 14% of the time, Pallas kernels for 39%

profile of v1, /device:TPU:0, one launch (start us, length us, event | category | flops | bytes accessed | tf_op | source)
XLA Modules:
  0.0 379.6 jit_solution(10255129972737056581)
XLA Ops:
  7.2 0.0 copy-start
  7.2 0.0 all-gather.3.cloned.1.call-start
  7.2 0.7 compare_select_fusion.1
  7.9 0.7 compare_and_fusion
  8.6 1.1 convert_element_type.28
  9.6 0.6 gather_fusion
  10.2 0.1 fusion.3
  10.3 0.2 reshape.128
  10.6 12.2 %all_to_all.18 = bf16[4,2,8192]{2,1,0:T(2,128)(2,1)S(1)} all-to-all(bf16[4,2,8192]{2,1,0:T(2,128)(2,1)S(1)} %reshape.128), channel_id=1, replica_groups=mesh['fsdp'=8,'tensor'=4] {'tensor'}, dimensions={0} | all-to-all | bytes 262144 | tf_op jit(solution)/shard_map/all_to_all | solution.py:237
  22.8 0.2 reshape.129
  23.0 0.2 copy.38
  23.2 0.9 all_to_all.16
  24.1 0.0 all-gather.3.cloned.1.call-update
  24.1 0.0 all-gather.5.cloned.1.call-start
  24.2 2.7 copy.37
  26.9 0.6 gather_fusion.2
  27.5 2.7 copy.36
  30.2 0.6 gather_fusion.3
  30.9 0.0 copy-start.3
  30.9 3.7 copy.35
  34.6 1.8 gather_fusion.4
  36.4 1.8 broadcast_select_fusion
  38.2 105.9 %spread.1 = (bf16[4096,1024]{1,0:T(8,128)(2,1)}, bf16[4096,1024]{1,0:T(8,128)(2,1)}, bf16[512,1024]{1,0:T(8,128)(2,1)}) custom-call(bf16[16,64,512]{2,1,0:T(8,128)(2,1)} %get-tuple-element.21.g0, bf16[16,64,512]{2,1,0:T(8,128)(2,1)} %get-tuple-element.20.g1, bf16[16,64,512]{2,1,0:T(8,128)(2,1)} %get-tuple-element.19.g2), custom_call_target="tpu_custom_call" | custom-call | tf_op jit(solution)/shard_map/spread/pallas_call | solution.py:184
  144.2 0.0 all-gather.5.cloned.1.call-update
  144.2 0.2 reduce-scatter.3.cloned.1.call-start
  144.4 0.0 copy-done.3
  144.5 0.1 compare_and_fusion.1
  144.5 0.0 copy-done
  144.6 0.6 gather_fusion.1
  145.1 0.7 fusion.2.r_ref
  145.8 0.0 copy-start.2
  145.8 15.1 %convolution_bitcast_fusion.pre_ref = f32[1024,1024]{1,0:T(8,128)} fusion(bf16[1024,4096]{1,0:T(8,128)(2,1)} %param.9, bf16[4096,1024]{1,0:T(8,128)(2,1)} %get-tuple-element.10.x_ref), kind=kOutput, calls=%fused_computation.7 | convolution fusion | flops 8589934592 | bytes 20971520 | tf_op jit(solution)/shard_map/dot_general | solution.py:255
  160.9 0.0 copy-done.2
  160.9 12.4 %convert_bitcast_fusion.x_ref = bf16[1024,1024]{1,0:T(8,128)(2,1)} fusion(bf16[1024,4096]{1,0:T(8,128)(2,1)} %param.9, bf16[4096,1024]{1,0:T(8,128)(2,1)S(1)} %copy-done.2), kind=kOutput, calls=%fused_computation.12 | convolution fusion | flops 8590983168 | bytes 18874368 | tf_op jit(solution)/shard_map/dot_general | solution.py:254
  173.3 0.0 all-gather.3.cloned.1.call-done
  173.3 2.4 copy.27.g_ref
  175.7 16.2 %recur.1 = bf16[1024,1024]{1,0:T(8,128)(2,1)} custom-call(bf16[1024,1024]{1,0:T(8,128)(2,1)} %convert_bitcast_fusion.x_ref, f32[1024,1024]{1,0:T(8,128)} %convolution_bitcast_fusion.pre_ref, bf16[2,4,256,256]{3,2,1,0:T(8,128)(2,1)} %copy.27.g_ref, f32[4,1,256]{2,1,0:T(1,128)} %fusion.2.r_ref), custom_call_target="tpu_custom_call" | custom-call | flops 1073741824 | bytes 8388608 | tf_op jit(solution)/shard_map/recur/pallas_call | solution.py:59
  191.9 0.0 copy-start.4
  191.9 11.5 %all-gather.5.cloned.1.call-done.x_ref = bf16[4096,1024]{1,0:T(8,128)(2,1)} async-done(((bf16[512,1024]{1,0:T(8,128)(2,1)}), bf16[4096,1024]{1,0:T(8,128)(2,1)}) %all-gather.5.cloned.1.call-update) | async-done | bytes 8388624 | tf_op jit(solution)/shard_map/all_gather | solution.py:252
  203.4 10.2 %convolution_convert_fusion.1 = bf16[512,4096]{1,0:T(8,128)(2,1)} fusion(bf16[4096,1024]{1,0:T(8,128)(2,1)} %all-gather.5.cloned.1.call-done.x_ref, bf16[1024,1024]{1,0:T(8,128)(2,1)} %recur.1), kind=kOutput, calls=%fused_computation.6 | convolution fusion | flops 4297064448 | bytes 13631488 | tf_op jit(solution)/shard_map/dot_general | solution.py:259
  213.6 0.0 reduce-scatter.3.cloned.1.call-update
  213.6 0.3 reduce-scatter.5.cloned.1.call-start
  213.9 0.0 copy-done.4
  213.9 9.5 %convolution_convert_fusion = bf16[512,4096]{1,0:T(8,128)(2,1)} fusion(bf16[4096,1024]{1,0:T(8,128)(2,1)} %all-gather.5.cloned.1.call-done.x_ref, bf16[1024,1024]{1,0:T(8,128)(2,1)S(1)} %copy-done.4), kind=kOutput, calls=%fused_computation.5 | convolution fusion | flops 4297064448 | bytes 13631488 | tf_op jit(solution)/shard_map/dot_general | solution.py:259
  223.3 0.0 reduce-scatter.5.cloned.1.call-update
  223.4 9.0 %dup.3 = bf16[4096,1024]{1,0:T(8,128)(2,1)} custom-call(bf16[4096,1024]{1,0:T(8,128)(2,1)} %get-tuple-element.9.x_ref), custom_call_target="tpu_custom_call" | custom-call | bytes 16777216 | tf_op jit(solution)/shard_map/dup/pallas_call | solution.py:212
  232.3 0.0 copy-start.1
  232.3 9.0 %dup.4 = bf16[4096,1024]{1,0:T(8,128)(2,1)} custom-call(bf16[4096,1024]{1,0:T(8,128)(2,1)} %get-tuple-element.10.x_ref), custom_call_target="tpu_custom_call" | custom-call | bytes 16777216 | tf_op jit(solution)/shard_map/dup/pallas_call | solution.py:212
  241.3 8.9 %dup.5 = bf16[4096,1024]{1,0:T(8,128)(2,1)} custom-call(bf16[4096,1024]{1,0:T(8,128)(2,1)} %all-gather.5.cloned.1.call-done.x_ref), custom_call_target="tpu_custom_call" | custom-call | bytes 16777216 | tf_op jit(solution)/shard_map/dup/pallas_call | solution.py:212
  250.3 40.3 %reduce-scatter.3.cloned.1.call-done = bf16[512,1024]{1,0:T(8,128)(2,1)} async-done(((bf16[512,4096]{1,0:T(8,128)(2,1)}), bf16[512,1024]{1,0:T(8,128)(2,1)}) %reduce-scatter.3.cloned.1.call-update) | async-done | bytes 1048592 | tf_op jit(solution)/shard_map/reduce_scatter | solution.py:263
  290.5 79.5 %reduce-scatter.5.cloned.1.call-done = bf16[512,1024]{1,0:T(8,128)(2,1)} async-done(((bf16[512,4096]{1,0:T(8,128)(2,1)}), bf16[512,1024]{1,0:T(8,128)(2,1)}) %reduce-scatter.5.cloned.1.call-update) | async-done | bytes 1048592 | tf_op jit(solution)/shard_map/reduce_scatter | solution.py:263
  370.0 3.0 pad_maximum_fusion
  373.0 0.0 copy-done.1
  (2 shorter events, 0.0 us)
Async XLA Ops:
  7.2 137.4 %copy-start = (f32[16,256]{1,0:T(8,128)S(1)}, f32[16,256]{1,0:T(8,128)}, u32[]{:S(2)}) copy-start(f32[16,256]{1,0:T(8,128)} %param.14) | copy-start | bytes 49156
  7.2 166.1 %all-gather.3.cloned.1.call-start = ((), (), s32[]{:S(2)}) async-start(), calls=%async_computation.3 | async-start | bytes 1179648 | tf_op jit(solution)/shard_map/all_gather | solution.py:239
  24.1 179.2 %all-gather.5.cloned.1.call-start = ((), (), s32[]{:S(2)}) async-start(), calls=%async_computation.4 | async-start | bytes 9437184 | tf_op jit(solution)/shard_map/all_gather | solution.py:252
  30.9 113.6 %copy-start.3 = (s32[16]{0:T(128)S(1)}, s32[16]{0:T(128)}, u32[]{:S(2)}) copy-start(s32[16]{0:T(128)} %param.15) | copy-start | bytes 196
  144.2 146.3 %reduce-scatter.3.cloned.1.call-start = ((), (), s32[]{:S(2)}) async-start(), calls=%async_computation.5 | async-start | bytes 5242880 | tf_op jit(solution)/shard_map/reduce_scatter | solution.py:263
  145.8 15.1 %copy-start.2 = (bf16[4096,1024]{1,0:T(8,128)(2,1)S(1)}, bf16[4096,1024]{1,0:T(8,128)(2,1)}, u32[]{:S(2)}) copy-start(bf16[4096,1024]{1,0:T(8,128)(2,1)} %get-tuple-element.9.x_ref) | copy-start | bytes 25165828
  191.9 22.0 %copy-start.4 = (bf16[1024,1024]{1,0:T(8,128)(2,1)S(1)}, bf16[1024,1024]{1,0:T(8,128)(2,1)}, u32[]{:S(2)}) copy-start(bf16[1024,1024]{1,0:T(8,128)(2,1)} %recur.1) | copy-start | bytes 6291460
  213.6 156.4 %reduce-scatter.5.cloned.1.call-start = ((), (), s32[]{:S(2)}) async-start(), calls=%async_computation.6 | async-start | bytes 5242880 | tf_op jit(solution)/shard_map/reduce_scatter | solution.py:263
  232.3 140.7 %copy-start.1 = (f32[16,256]{1,0:T(8,128)S(1)}, f32[16,256]{1,0:T(8,128)}, u32[]{:S(2)}) copy-start(f32[16,256]{1,0:T(8,128)} %param.14) | copy-start | bytes 49156
Sparse Core Ops, SparseCore 0:
  24.3 22.4 all-gather.2
  144.3 58.9 all-gather.4
  213.7 76.7 reduce-scatter.2
  292.7 77.2 reduce-scatter.4

commit v2 on v1

--- a/solution.py
+++ b/solution.py
@@ -80,16 +80,20 @@
     )(branch_in, gate_pre, gates, rate)
 
 
-def spread_body(g0, g1, g2, out0, out1, piece2, held, piece, own_sem, z_send, z_recv, put_sem, f_send, f_recv):
-    gs, outs = (g0, g1, g2), (out0, out1)
+def spread_body(
+    g0, g1, g2, gg, out0, out1, piece2, gates_out,
+    held, piece, gheld, gpiece, gfull, own_sem, z_send, z_recv, put_sem, f_send, f_recv,
+):
+    gs = (g0, g1, g2)
     z, f = lax.axis_index("tensor"), lax.axis_index("fsdp")
-    zs = held.shape[1]
-    per = held.shape[2]
-    rows = piece.shape[1]
-    half = rows // 2
+    zs, per = held.shape[1], held.shape[2]
+    half = piece.shape[1]
+    rows = 2 * half
+    ghalf = gpiece.shape[3]
     sib = f + 1 - 2 * (f % 2)
     xp = f + 2 - 4 * ((f // 2) % 2)
     yp = f + 4 - 8 * (f // 4)
+    diag = xp + 4 - 8 * (xp // 4)
 
     barrier = pltpu.get_barrier_semaphore()
     for peer in (sib, xp, yp):
@@ -100,105 +104,169 @@
         )
     pl.semaphore_wait(barrier, 3 + zs - 1)
 
+    def z_source(q, to):
+        if q == 6:
+            return gg.at[:, pl.ds(to * per, per)]
+        return gs[q // 2].at[pl.ds(to * per, per), :, pl.ds((q % 2) * half, half)]
+
+    def z_target(q):
+        if q == 6:
+            return gheld.at[z]
+        return held.at[q // 2, z, :, :, pl.ds((q % 2) * half, half)]
+
     a2a, own = {}, {}
-    for w in range(3):
+    for q in (0, 1, 2, 6, 3, 4, 5):
         for k in range(1, zs):
             to = (z + k) % zs
-            a2a[w, k] = pltpu.make_async_remote_copy(
-                src_ref=gs[w].at[pl.ds(to * per, per)],
-                dst_ref=held.at[w, z],
-                send_sem=z_send.at[w, k],
-                recv_sem=z_recv.at[w, k],
+            a2a[q, k] = pltpu.make_async_remote_copy(
+                src_ref=z_source(q, to),
+                dst_ref=z_target(q),
+                send_sem=z_send.at[q, k],
+                recv_sem=z_recv.at[q, k],
                 device_id={"tensor": to},
                 device_id_type=MESH,
             )
-            a2a[w, k].start()
-        own[w] = pltpu.make_async_copy(gs[w].at[pl.ds(z * per, per)], held.at[w, z], own_sem.at[w])
-        own[w].start()
-
-    def assemble(w, dst):
-        own[w].wait()
+            a2a[q, k].start()
+        own[q] = pltpu.make_async_copy(z_source(q, z), z_target(q), own_sem.at[q])
+        own[q].start()
+
+    def arrive(q):
+        own[q].wait()
         for k in range(1, zs):
-            a2a[w, k].wait_recv()
+            a2a[q, k].wait_recv()
+
+    def assemble(q, dst):
+        arrive(q)
+        at = slice((q % 2) * half, (q % 2) * half + half)
         for b in range(per):
-            slab = jnp.concatenate([held[w, s, b] for s in range(zs)], axis=0)
+            slab = jnp.concatenate([held[q // 2, s, b, :, at] for s in range(zs)], axis=0)
             width = slab.shape[0]
             dst[:, b * width : (b + 1) * width] = slab.T
 
-    sent = {}
-
-    def send(w, i, src, start, count, peer):
-        at = outs[w].at[pl.ds(start, count)]
-        sent[w, i] = pltpu.make_async_remote_copy(
+    def view(q, owner):
+        if q >= 4:
+            return gfull.at[:, :, pl.ds(owner * 2 * ghalf + (q - 4) * ghalf, ghalf)]
+        return (out0, out1)[q // 2].at[pl.ds(owner * rows + (q % 2) * half, half)]
+
+    sent, put = {}, {}
+
+    def send(q, i, src, owner, peer):
+        at = view(q, owner)
+        sent[q, i] = pltpu.make_async_remote_copy(
             src_ref=at if src is None else src,
             dst_ref=at,
-            send_sem=f_send.at[w, i],
-            recv_sem=f_recv.at[w, i],
+            send_sem=f_send.at[q, i],
+            recv_sem=f_recv.at[q, i],
             device_id={"fsdp": peer},
             device_id_type=MESH,
         )
-        sent[w, i].start()
-
-    put = {}
-    diag = xp + 4 - 8 * (xp // 4)
-    for w in range(2):
-        assemble(w, piece.at[w])
-        send(w, 0, piece.at[w], f * rows, rows, xp)
-        send(w, 1, piece.at[w], f * rows, rows, yp)
-        send(w, 2, piece.at[w], f * rows, rows, sib)
-        put[w] = pltpu.make_async_copy(piece.at[w], outs[w].at[pl.ds(f * rows, rows)], put_sem.at[w])
-        put[w].start()
-    for w in range(2):
-        sent[w, 0].wait_recv()
-        send(w, 3, None, xp * rows, half, yp)
-        send(w, 4, None, xp * rows, rows, sib)
-        sent[w, 1].wait_recv()
-        send(w, 5, None, yp * rows + half, half, xp)
-        send(w, 6, None, yp * rows, rows, sib)
-        if w == 0:
-            assemble(2, piece2)
-    for w in range(2):
-        sent[w, 3].wait_recv()
-        send(w, 7, None, diag * rows, half, sib)
-        sent[w, 5].wait_recv()
-        send(w, 8, None, diag * rows + half, half, sib)
-    for w in range(2):
-        for i in (2, 4, 6, 7, 8):
-            sent[w, i].wait_recv()
-        for i in range(9):
-            sent[w, i].wait_send()
-        put[w].wait()
-    for w in range(3):
+        sent[q, i].start()
+
+    def first(q):
+        if q >= 4:
+            src = gpiece.at[q - 4]
+        else:
+            src = piece.at[q]
+            assemble(q, src)
+        for i, peer in enumerate((xp, yp, sib)):
+            send(q, i, src, f, peer)
+        put[q] = pltpu.make_async_copy(src, view(q, f), put_sem.at[q])
+        put[q].start()
+
+    def relay(q):
+        sent[q, 0].wait_recv()
+        if q % 2 == 0:
+            send(q, 3, None, xp, yp)
+        send(q, 4, None, xp, sib)
+        sent[q, 1].wait_recv()
+        if q % 2 == 1:
+            send(q, 3, None, yp, xp)
+        send(q, 5, None, yp, sib)
+
+    def across(q):
+        sent[q, 3].wait_recv()
+        send(q, 6, None, diag, sib)
+
+    first(0)
+    first(1)
+    relay(0)
+    first(2)
+    arrive(6)
+    for h in range(2):
+        for g in range(gpiece.shape[1]):
+            for b in range(per):
+                gpiece[h, g, b] = jnp.concatenate(
+                    [gheld[s, g, b, h * ghalf : (h + 1) * ghalf, :] for s in range(zs)], axis=1
+                )
+    first(4)
+    first(5)
+    relay(1)
+    first(3)
+    across(0)
+    relay(2)
+    relay(4)
+    relay(5)
+    assemble(4, piece2.at[pl.ds(0, half)])
+    across(1)
+    relay(3)
+    assemble(5, piece2.at[pl.ds(half, half)])
+    for q in (4, 5, 2, 3):
+        across(q)
+    for q in (4, 5):
+        for i in (2, 4, 5, 6):
+            sent[q, i].wait_recv()
+        put[q].wait()
+    for g in range(gfull.shape[0]):
+        for b in range(per):
+            gates_out[g, b] = gfull[g, b].T
+    for q in range(4):
+        for i in (2, 4, 5, 6):
+            sent[q, i].wait_recv()
+        put[q].wait()
+    for q in range(6):
+        for i in range(7):
+            sent[q, i].wait_send()
+    for q in range(7):
         for k in range(1, zs):
-            a2a[w, k].wait_send()
-
-
-def spread(groups, zs, fs):
+            a2a[q, k].wait_send()
+
+
+def spread(groups, gates, zs, fs):
     blocks, chan, rows = groups[0].shape
+    kinds, _, gin, gout = gates.shape
     per = blocks // zs
     width = per * chan * zs
     full = jax.ShapeDtypeStruct((rows * fs, width), jnp.bfloat16)
+    square = (kinds, per, gin * fs, gout * zs)
     vmem = pl.BlockSpec(memory_space=pltpu.VMEM)
     hbm = pl.BlockSpec(memory_space=pl.ANY)
     dma = pltpu.SemaphoreType.DMA
     return pl.pallas_call(
         spread_body,
-        in_specs=[vmem] * 3,
-        out_specs=[hbm, hbm, vmem],
-        out_shape=[full, full, jax.ShapeDtypeStruct((rows, width), jnp.bfloat16)],
+        in_specs=[vmem] * 4,
+        out_specs=[hbm, hbm, vmem, vmem],
+        out_shape=[
+            full,
+            full,
+            jax.ShapeDtypeStruct((rows, width), jnp.bfloat16),
+            jax.ShapeDtypeStruct((kinds, per, gout * zs, gin * fs), jnp.bfloat16),
+        ],
         scratch_shapes=[
             pltpu.VMEM((3, zs, per, chan, rows), jnp.bfloat16),
-            pltpu.VMEM((2, rows, width), jnp.bfloat16),
-            dma((3,)),
-            dma((3, zs)),
-            dma((3, zs)),
-            dma((2,)),
-            dma((2, 9)),
-            dma((2, 9)),
+            pltpu.VMEM((4, rows // 2, width), jnp.bfloat16),
+            pltpu.VMEM((zs, kinds, per, gin, gout), jnp.bfloat16),
+            pltpu.VMEM((2, kinds, per, gin // 2, gout * zs), jnp.bfloat16),
+            pltpu.VMEM(square, jnp.bfloat16),
+            dma((7,)),
+            dma((7, zs)),
+            dma((7, zs)),
+            dma((6,)),
+            dma((6, 7)),
+            dma((6, 7)),
         ],
         compiler_params=pltpu.CompilerParams(collective_id=0, has_side_effects=True),
         name="spread",
-    )(*groups)
+    )(*groups, gates)
 
 
 def dup_body(x_ref, o_ref):
@@ -234,14 +302,16 @@
     gate_cast = gates_source.astype(jnp.bfloat16)
     sectioned = tuple((jnp.take(weight, block_order, axis=1) for weight in casted))
     gate_sectioned = jnp.take(gate_cast, block_order, axis=1)
-    gate_group = lax.all_to_all(gate_sectioned, "tensor", split_axis=1, concat_axis=3, tiled=True)
-    gate_piece = jnp.transpose(gate_group, (0, 1, 3, 2))
-    gates_serve = lax.all_gather(gate_piece, "fsdp", axis=3, tiled=True)
     row_count = tokens.shape[0]
     if lax.axis_size("fsdp") == 8:
         groups = [jnp.transpose(weight, (1, 0, 2)) for weight in sectioned]
-        input_serve, branch_serve, output_piece = spread(groups, tensor_count, 8)
+        input_serve, branch_serve, output_piece, gates_serve = spread(
+            groups, gate_sectioned, tensor_count, 8
+        )
     else:
+        gate_group = lax.all_to_all(gate_sectioned, "tensor", split_axis=1, concat_axis=3, tiled=True)
+        gate_piece = jnp.transpose(gate_group, (0, 1, 3, 2))
+        gates_serve = lax.all_gather(gate_piece, "fsdp", axis=3, tiled=True)
         regrouped = lax.all_to_all(sectioned, "tensor", split_axis=1, concat_axis=0, tiled=True)
         pieces = tuple(
             (jnp.transpose(weight, (2, 1, 0)).reshape(weight.shape[2], -1) for weight in regrouped)
@@ -255,7 +325,7 @@
     gate_pre = jnp.dot(tokens, branch_serve, preferred_element_type=jnp.float32)
     gated = recur(branch_in, gate_pre, gates_serve, rate, row_count // LEN)
     parts = []
-    for rows in jnp.split(gated, 2, axis=0):
+    for rows in jnp.split(gated, [row_count // 8], axis=0):
         partial_value = lax.dot_general(
             rows, output_serve, (((1,), (1,)), ((), ())), preferred_element_type=jnp.float32
         )

time: 381 us -> 371 us (0.974)
  blocking collectives: 12.2 us -> 0 us
    all_to_all x1 -> x0, blocking collectives: 12.2 us -> none  [on_device(): lax.all_to_all(gate_sectioned, 'tensor', split_axis=1, concat_axis=3, til...]
    all_gather x1, waiting for transfers between devices: 11.5 us -> 17 us  [on_device(): output_serve = lax.all_gather(output_piece, 'fsdp', axis=0, tiled=True)]
    reduce_scatter x2, waiting for transfers between devices: 120 us -> 116 us  [on_device(): lax.psum_scatter(partial_value.astype(jnp.bfloat16), 'tensor', scatter_di...]
    unnamed x15 -> x16, local copies, waits for them, and re-layouts: 9.6 us -> 10.1 us
  transfers between devices with their start and end apart: 4 -> 3, of which waited for: 3 -> 2; matrix products, arithmetic and copies ran while one was open for 14% -> 11% of each run, Pallas kernels for 39% -> 12%
where the time goes in v2:
time: 371 us; the launch traced here: 370 us
  Pallas kernels  150 us (40%)
  waiting for transfers between devices  133 us (36%)
  matrix products  48.3 us (13%)
  local copies, waits for them, and re-layouts  15 us (4%)
  between operations  13.8 us (4%)
  other arithmetic  9.74 us (3%)
    reduce_scatter x2, waiting for transfers between devices, on_device(): lax.psum_scatter(partial_value.astype(jnp.bfloat16), 'tensor', scatter_di...  116 us
    pallas_call x1, Pallas kernels, spread(): pl.pallas_call(spread_body, in_specs=[vmem] * 4, out_specs=[hbm, hbm, vme...  106 us
    pallas_call x3, Pallas kernels, dup(): pl.pallas_call(dup_body, grid=(rows // tile,), in_specs=[spec], out_specs...  27.1 us
    dot_general x2, matrix products, on_device(): lax.dot_general(rows, output_serve, (((1,), (1,)), ((), ())), preferred_e...  20.5 us
    all_gather x1, waiting for transfers between devices, on_device(): output_serve = lax.all_gather(output_piece, 'fsdp', axis=0, tiled=True)  17 us
    pallas_call x1, Pallas kernels, recur(): pl.pallas_call(functools.partial(recur_body, prompts), grid=(blocks, rows...  16.5 us
    dot_general x1, matrix products, on_device(): gate_pre = jnp.dot(tokens, branch_serve, preferred_element_type=jnp.float32)  15.1 us
    dot_general x1, matrix products, on_device(): jnp.dot(tokens, input_serve, preferred_element_type=jnp.float32)  12.7 us
  transfers between devices with their start and end apart: 3, of which 2 were waited for; matrix products, arithmetic and copies ran while one was open for 11% of the time, Pallas kernels for 12%

profile of v2, /device:TPU:0, one launch (start us, length us, event | category | flops | bytes accessed | tf_op | source)
XLA Modules:
  0.0 369.8 jit_solution(6447066490654464036)
XLA Ops:
  7.2 0.0 copy-start
  7.2 0.0 all-gather.2.cloned.1.call-start
  7.2 0.7 compare_select_fusion.1
  7.9 0.7 compare_and_fusion
  8.6 2.7 copy.30
  11.3 2.7 copy.29
  14.0 0.6 gather_fusion.2
  14.6 0.6 gather_fusion.3
  15.2 3.7 copy.28
  18.9 0.0 copy-start.5
  18.9 1.9 gather_fusion.4
  20.8 1.1 convert_element_type.26
  21.9 1.3 gather_fusion
  23.1 1.7 fusion.2.gg
  24.9 1.8 broadcast_select_fusion
  26.7 106.2 %spread.1 = (bf16[4096,1024]{1,0:T(8,128)(2,1)}, bf16[4096,1024]{1,0:T(8,128)(2,1)}, bf16[512,1024]{1,0:T(8,128)(2,1)}, bf16[2,4,256,256]{3,2,1,0:T(8,128)(2,1)}) custom-call(bf16[16,64,512]{2,1,0:T(8,128)(2,1)} %get-tuple-element.18.g0, bf16[16,64,512]{2,1,0:T(8,128)(2,1)} %get-tuple-element.17.g1, bf16[16,64,512]{2,1,0:T(8,128)(2,1)} %get-tuple-element.16.g2, ...), custom_call_target="tpu_custom_call" | custom-call | tf_op jit(solution)/shard_map/spread/pallas_call | solution.py:244
  133.0 0.0 all-gather.2.cloned.1.call-update
  133.0 0.2 reduce-scatter.3.cloned.1.call-start
  133.2 0.0 copy-done.5
  133.2 0.1 compare_and_fusion.1
  133.3 0.0 copy-done
  133.3 0.6 gather_fusion.1
  133.9 0.7 fusion.3.r_ref
  134.6 0.0 copy-start.2
  134.6 15.1 %convolution_bitcast_fusion.pre_ref = f32[1024,1024]{1,0:T(8,128)} fusion(bf16[1024,4096]{1,0:T(8,128)(2,1)} %param.9, bf16[4096,1024]{1,0:T(8,128)(2,1)} %get-tuple-element.11.x_ref), kind=kOutput, calls=%fused_computation.7 | convolution fusion | flops 8589934592 | bytes 20971520 | tf_op jit(solution)/shard_map/dot_general | solution.py:325
  149.7 0.0 copy-done.2
  149.7 12.7 %convert_bitcast_fusion.x_ref = bf16[1024,1024]{1,0:T(8,128)(2,1)} fusion(bf16[1024,4096]{1,0:T(8,128)(2,1)} %param.9, bf16[4096,1024]{1,0:T(8,128)(2,1)S(1)} %copy-done.2), kind=kOutput, calls=%fused_computation.12 | convolution fusion | flops 8590983168 | bytes 18874368 | tf_op jit(solution)/shard_map/dot_general | solution.py:324
  162.4 16.5 %recur.1 = bf16[1024,1024]{1,0:T(8,128)(2,1)} custom-call(bf16[1024,1024]{1,0:T(8,128)(2,1)} %convert_bitcast_fusion.x_ref, f32[1024,1024]{1,0:T(8,128)} %convolution_bitcast_fusion.pre_ref, bf16[2,4,256,256]{3,2,1,0:T(8,128)(2,1)} %get-tuple-element.28.g_ref, f32[4,1,256]{2,1,0:T(1,128)} %fusion.3.r_ref), custom_call_target="tpu_custom_call" | custom-call | flops 1073741824 | bytes 8388608 | tf_op jit(solution)/shard_map/recur/pallas_call | solution.py:59
  178.8 0.0 copy-start.4
  178.8 17.0 %all-gather.2.cloned.1.call-done.x_ref = bf16[4096,1024]{1,0:T(8,128)(2,1)} async-done(((bf16[512,1024]{1,0:T(8,128)(2,1)}), bf16[4096,1024]{1,0:T(8,128)(2,1)}) %all-gather.2.cloned.1.call-update) | async-done | bytes 8388624 | tf_op jit(solution)/shard_map/all_gather | solution.py:322
  195.9 7.3 %convolution_convert_fusion.1 = bf16[128,4096]{1,0:T(8,128)(2,1)} fusion(bf16[4096,1024]{1,0:T(8,128)(2,1)} %all-gather.2.cloned.1.call-done.x_ref, bf16[1024,1024]{1,0:T(8,128)(2,1)} %recur.1), kind=kOutput, calls=%fused_computation.6 | convolution fusion | flops 1074266112 | bytes 9699328 | tf_op jit(solution)/shard_map/dot_general | solution.py:329
  203.2 0.0 reduce-scatter.3.cloned.1.call-update
  203.2 0.0 reduce-scatter.5.cloned.1.call-start
  203.3 0.0 copy-done.4
  203.3 13.1 %convolution_convert_fusion = bf16[896,4096]{1,0:T(8,128)(2,1)} fusion(bf16[4096,1024]{1,0:T(8,128)(2,1)} %all-gather.2.cloned.1.call-done.x_ref, bf16[1024,1024]{1,0:T(8,128)(2,1)S(1)} %copy-done.4), kind=kOutput, calls=%fused_computation.5 | convolution fusion | flops 7519862784 | bytes 17563648 | tf_op jit(solution)/shard_map/dot_general | solution.py:329
  216.4 0.0 reduce-scatter.5.cloned.1.call-update
  216.5 9.0 %dup.3 = bf16[4096,1024]{1,0:T(8,128)(2,1)} custom-call(bf16[4096,1024]{1,0:T(8,128)(2,1)} %get-tuple-element.10.x_ref), custom_call_target="tpu_custom_call" | custom-call | bytes 16777216 | tf_op jit(solution)/shard_map/dup/pallas_call | solution.py:280
  225.4 9.0 %dup.4 = bf16[4096,1024]{1,0:T(8,128)(2,1)} custom-call(bf16[4096,1024]{1,0:T(8,128)(2,1)} %get-tuple-element.11.x_ref), custom_call_target="tpu_custom_call" | custom-call | bytes 16777216 | tf_op jit(solution)/shard_map/dup/pallas_call | solution.py:280
  234.4 0.0 copy-start.3
  234.4 0.0 copy-start.1
  234.4 9.2 %dup.5 = bf16[4096,1024]{1,0:T(8,128)(2,1)} custom-call(bf16[4096,1024]{1,0:T(8,128)(2,1)} %all-gather.2.cloned.1.call-done.x_ref), custom_call_target="tpu_custom_call" | custom-call | bytes 16777216 | tf_op jit(solution)/shard_map/dup/pallas_call | solution.py:280
  243.6 0.0 reduce-scatter.3.cloned.1.call-done
  243.6 115.7 %reduce-scatter.5.cloned.1.call-done = bf16[896,1024]{1,0:T(8,128)(2,1)} async-done(((bf16[896,4096]{1,0:T(8,128)(2,1)}), bf16[896,1024]{1,0:T(8,128)(2,1)}) %reduce-scatter.5.cloned.1.call-update) | async-done | bytes 1835024 | tf_op jit(solution)/shard_map/reduce_scatter | solution.py:333
  359.3 3.0 pad_maximum_fusion
  362.3 0.0 copy-done.3
  362.3 1.0 copy.32
  363.3 0.0 copy-done.1
  (2 shorter events, 0.0 us)
Async XLA Ops:
  7.2 126.2 %copy-start = (f32[16,256]{1,0:T(8,128)S(1)}, f32[16,256]{1,0:T(8,128)}, u32[]{:S(2)}) copy-start(f32[16,256]{1,0:T(8,128)} %param.14) | copy-start | bytes 49156
  7.2 188.7 %all-gather.2.cloned.1.call-start = ((), (), s32[]{:S(2)}) async-start(), calls=%async_computation.2 | async-start | bytes 9437184 | tf_op jit(solution)/shard_map/all_gather | solution.py:322
  18.9 114.3 %copy-start.5 = (s32[16]{0:T(128)S(1)}, s32[16]{0:T(128)}, u32[]{:S(2)}) copy-start(s32[16]{0:T(128)} %param.15) | copy-start | bytes 196
  133.0 110.6 %reduce-scatter.3.cloned.1.call-start = ((), (), s32[]{:S(2)}) async-start(), calls=%async_computation.3 | async-start | bytes 1310720 | tf_op jit(solution)/shard_map/reduce_scatter | solution.py:333
  134.6 15.1 %copy-start.2 = (bf16[4096,1024]{1,0:T(8,128)(2,1)S(1)}, bf16[4096,1024]{1,0:T(8,128)(2,1)}, u32[]{:S(2)}) copy-start(bf16[4096,1024]{1,0:T(8,128)(2,1)} %get-tuple-element.10.x_ref) | copy-start | bytes 25165828
  178.8 24.5 %copy-start.4 = (bf16[1024,1024]{1,0:T(8,128)(2,1)S(1)}, bf16[1024,1024]{1,0:T(8,128)(2,1)}, u32[]{:S(2)}) copy-start(bf16[1024,1024]{1,0:T(8,128)(2,1)} %recur.1) | copy-start | bytes 6291460
  203.2 156.1 %reduce-scatter.5.cloned.1.call-start = ((), (), s32[]{:S(2)}) async-start(), calls=%async_computation.4 | async-start | bytes 9175040 | tf_op jit(solution)/shard_map/reduce_scatter | solution.py:333
  234.4 127.9 %copy-start.3 = (bf16[2,4,256,256]{3,2,1,0:T(8,128)(2,1)S(1)}, bf16[2,4,256,256]{3,2,1,0:T(8,128)(2,1)}, u32[]{:S(2)}) copy-start(bf16[2,4,256,256]{3,2,1,0:T(8,128)(2,1)} %get-tuple-element.28.g_ref) | copy-start | bytes 3145732
  234.4 128.8 %copy-start.1 = (f32[16,256]{1,0:T(8,128)S(1)}, f32[16,256]{1,0:T(8,128)}, u32[]{:S(2)}) copy-start(f32[16,256]{1,0:T(8,128)} %param.14) | copy-start | bytes 49156
Sparse Core Ops, SparseCore 0:
  133.1 62.7 all-gather.1
  203.3 27.2 reduce-scatter.2
  233.0 126.2 reduce-scatter.4

commit v3 on v2

--- a/solution.py
+++ b/solution.py
@@ -115,7 +115,10 @@
         return held.at[q // 2, z, :, :, pl.ds((q % 2) * half, half)]
 
     a2a, own = {}, {}
-    for q in (0, 1, 2, 6, 3, 4, 5):
+    queue = [0, 1, 2, 6, 3, 4, 5]
+
+    def depart():
+        q = queue.pop(0)
         for k in range(1, zs):
             to = (z + k) % zs
             a2a[q, k] = pltpu.make_async_remote_copy(
@@ -130,10 +133,15 @@
         own[q] = pltpu.make_async_copy(z_source(q, z), z_target(q), own_sem.at[q])
         own[q].start()
 
+    depart()
+    depart()
+
     def arrive(q):
         own[q].wait()
         for k in range(1, zs):
             a2a[q, k].wait_recv()
+        if queue:
+            depart()
 
     def assemble(q, dst):
         arrive(q)
@@ -300,8 +308,8 @@
         output_source.astype(jnp.bfloat16),
     )
     gate_cast = gates_source.astype(jnp.bfloat16)
-    sectioned = tuple((jnp.take(weight, block_order, axis=1) for weight in casted))
-    gate_sectioned = jnp.take(gate_cast, block_order, axis=1)
+    sectioned = tuple((jnp.take(weight, block_order, axis=1, mode="clip") for weight in casted))
+    gate_sectioned = jnp.take(gate_cast, block_order, axis=1, mode="clip")
     row_count = tokens.shape[0]
     if lax.axis_size("fsdp") == 8:
         groups = [jnp.transpose(weight, (1, 0, 2)) for weight in sectioned]
@@ -320,21 +328,16 @@
         branch_serve = lax.all_gather(pieces[1], "fsdp", axis=0, tiled=True)
         output_piece = pieces[2]
     output_serve = lax.all_gather(output_piece, "fsdp", axis=0, tiled=True)
-    rate = -8.0 * jax.nn.softplus(jnp.take(decay_param, own_blocks, axis=0))[:, None, :]
+    rate = -8.0 * jax.nn.softplus(jnp.take(decay_param, own_blocks, axis=0, mode="clip"))[:, None, :]
     branch_in = jnp.dot(tokens, input_serve, preferred_element_type=jnp.float32).astype(jnp.bfloat16)
     gate_pre = jnp.dot(tokens, branch_serve, preferred_element_type=jnp.float32)
     gated = recur(branch_in, gate_pre, gates_serve, rate, row_count // LEN)
-    parts = []
-    for rows in jnp.split(gated, [row_count // 8], axis=0):
-        partial_value = lax.dot_general(
-            rows, output_serve, (((1,), (1,)), ((), ())), preferred_element_type=jnp.float32
-        )
-        parts.append(
-            lax.psum_scatter(
-                partial_value.astype(jnp.bfloat16), "tensor", scatter_dimension=1, tiled=True
-            )
-        )
-    mixed = jnp.concatenate(parts, axis=0)
+    partial_value = lax.dot_general(
+        gated, output_serve, (((1,), (1,)), ((), ())), preferred_element_type=jnp.float32
+    )
+    mixed = lax.psum_scatter(
+        partial_value.astype(jnp.bfloat16), "tensor", scatter_dimension=1, tiled=True
+    )
     return (mixed, dup(input_serve), dup(branch_serve), dup(output_serve), gates_serve)
 
 

time: 371 us -> 348 us (0.938)
  other arithmetic: 9.74 us -> 1.38 us
  matrix products: 48.3 us -> 42.2 us
  Pallas kernels: 150 us -> 144 us
  waiting for transfers between devices: 133 us -> 129 us
    all_gather x1, waiting for transfers between devices: 17 us -> 11 us  [on_device(): output_serve = lax.all_gather(output_piece, 'fsdp', axis=0, tiled=True)]
    dot_general x2 -> x1, matrix products: 20.5 us -> 14.7 us  [on_device(): lax.dot_general(gated, output_serve, (((1,), (1,)), ((), ())), preferred_...]
    pallas_call x1, Pallas kernels: 106 us -> 101 us  [spread(): pl.pallas_call(spread_body, in_specs=[vmem] * 4, out_specs=[hbm, hbm, vme...]
    select_n x3 -> x0, other arithmetic: 4.23 us -> none  [the longest x2 2.49 us: on_device(): jnp.take(weight, block_order, axis=1)]
    reduce_scatter x2 -> x1, waiting for transfers between devices: 116 us -> 118 us  [on_device(): lax.psum_scatter(partial_value.astype(jnp.bfloat16), 'tensor', scatter_di...]
  transfers between devices with their start and end apart: 3 -> 2, of which waited for: 2 -> 2; matrix products, arithmetic and copies ran while one was open for 11% -> 8% of each run, Pallas kernels for 12% -> 13%
where the time goes in v3:
time: 348 us; the launch traced here: 347 us
  Pallas kernels  144 us (41%)
  waiting for transfers between devices  129 us (37%)
  matrix products  42.2 us (12%)
  local copies, waits for them, and re-layouts  15.8 us (5%)
  between operations  14.1 us (4%)
    reduce_scatter x1, waiting for transfers between devices, on_device(): lax.psum_scatter(partial_value.astype(jnp.bfloat16), 'tensor', scatter_di...  118 us
    pallas_call x1, Pallas kernels, spread(): pl.pallas_call(spread_body, in_specs=[vmem] * 4, out_specs=[hbm, hbm, vme...  101 us
    pallas_call x3, Pallas kernels, dup(): pl.pallas_call(dup_body, grid=(rows // tile,), in_specs=[spec], out_specs...  27.1 us
    pallas_call x1, Pallas kernels, recur(): pl.pallas_call(functools.partial(recur_body, prompts), grid=(blocks, rows...  16.4 us
    dot_general x1, matrix products, on_device(): gate_pre = jnp.dot(tokens, branch_serve, preferred_element_type=jnp.float32)  15.1 us
    dot_general x1, matrix products, on_device(): lax.dot_general(gated, output_serve, (((1,), (1,)), ((), ())), preferred_...  14.7 us
    dot_general x1, matrix products, on_device(): jnp.dot(tokens, input_serve, preferred_element_type=jnp.float32)  12.4 us
    all_gather x1, waiting for transfers between devices, on_device(): output_serve = lax.all_gather(output_piece, 'fsdp', axis=0, tiled=True)  11 us
  transfers between devices with their start and end apart: 2, of which 2 were waited for; matrix products, arithmetic and copies ran while one was open for 8% of the time, Pallas kernels for 13%

profile of v3, /device:TPU:0, one launch (start us, length us, event | category | flops | bytes accessed | tf_op | source)
XLA Modules:
  0.0 346.5 jit_solution(1610965338638643076)
XLA Ops:
  7.2 0.0 copy-start
  7.2 0.0 copy-start.4
  7.2 0.0 all-gather.2.cloned.1.call-start
  7.2 0.7 pad_clamp_fusion.1
  8.0 2.7 copy.22
  10.7 2.7 copy.21
  13.4 0.0 copy-start.5
  13.4 1.6 gather_fusion
  15.0 1.6 gather_fusion.1
  16.5 2.7 copy.20
  19.3 1.6 gather_fusion.2
  20.8 0.0 copy-done.4
  20.9 0.6 gather_fusion.3
  21.5 0.7 copy.23
  22.2 100.5 %spread.1 = (bf16[4096,1024]{1,0:T(8,128)(2,1)}, bf16[4096,1024]{1,0:T(8,128)(2,1)}, bf16[512,1024]{1,0:T(8,128)(2,1)}, bf16[2,4,256,256]{3,2,1,0:T(8,128)(2,1)}) custom-call(bf16[16,64,512]{2,1,0:T(8,128)(2,1)} %gather_fusion, bf16[16,64,512]{2,1,0:T(8,128)(2,1)} %gather_fusion.1, bf16[16,64,512]{2,1,0:T(8,128)(2,1)} %gather_fusion.2, ...), custom_call_target="tpu_custom_call" | custom-call | tf_op jit(solution)/shard_map/spread/pallas_call | solution.py:252
  122.7 0.0 all-gather.2.cloned.1.call-update
  122.8 0.2 reduce-scatter.2.cloned.1.call-start
  123.0 0.0 copy-done.5
  123.0 0.1 dynamic_slice.3
  123.1 0.0 copy-done
  123.1 0.6 gather_fusion.4
  123.7 0.6 fusion.r_ref
  124.3 0.0 copy-start.2
  124.3 15.1 %convolution_bitcast_fusion.pre_ref = f32[1024,1024]{1,0:T(8,128)} fusion(bf16[1024,4096]{1,0:T(8,128)(2,1)} %param.7, bf16[4096,1024]{1,0:T(8,128)(2,1)} %get-tuple-element.10.x_ref), kind=kOutput, calls=%fused_computation.6 | convolution fusion | flops 8589934592 | bytes 20971520 | tf_op jit(solution)/shard_map/dot_general | solution.py:333
  139.4 0.0 copy-done.2
  139.4 12.4 %convert_bitcast_fusion.x_ref = bf16[1024,1024]{1,0:T(8,128)(2,1)} fusion(bf16[1024,4096]{1,0:T(8,128)(2,1)} %param.7, bf16[4096,1024]{1,0:T(8,128)(2,1)S(1)} %copy-done.2), kind=kOutput, calls=%fused_computation.10 | convolution fusion | flops 8590983168 | bytes 18874368 | tf_op jit(solution)/shard_map/dot_general | solution.py:332
  151.7 16.4 %recur.1 = bf16[1024,1024]{1,0:T(8,128)(2,1)} custom-call(bf16[1024,1024]{1,0:T(8,128)(2,1)} %convert_bitcast_fusion.x_ref, f32[1024,1024]{1,0:T(8,128)} %convolution_bitcast_fusion.pre_ref, bf16[2,4,256,256]{3,2,1,0:T(8,128)(2,1)} %get-tuple-element.22.g_ref, f32[4,1,256]{2,1,0:T(1,128)} %fusion.r_ref), custom_call_target="tpu_custom_call" | custom-call | flops 1073741824 | bytes 8388608 | tf_op jit(solution)/shard_map/recur/pallas_call | solution.py:59
  168.1 11.0 %all-gather.2.cloned.1.call-done.x_ref = bf16[4096,1024]{1,0:T(8,128)(2,1)} async-done(((bf16[512,1024]{1,0:T(8,128)(2,1)}), bf16[4096,1024]{1,0:T(8,128)(2,1)}) %all-gather.2.cloned.1.call-update) | async-done | bytes 8388624 | tf_op jit(solution)/shard_map/all_gather | solution.py:330
  179.2 14.7 %convolution_convert_fusion = bf16[1024,4096]{1,0:T(8,128)(2,1)} fusion(bf16[1024,1024]{1,0:T(8,128)(2,1)} %recur.1, bf16[4096,1024]{1,0:T(8,128)(2,1)} %all-gather.2.cloned.1.call-done.x_ref), kind=kOutput, calls=%fused_computation.5 | convolution fusion | flops 8594128896 | bytes 18874368 | tf_op jit(solution)/shard_map/dot_general | solution.py:335
  193.9 0.0 reduce-scatter.2.cloned.1.call-update
  193.9 9.0 %dup.3 = bf16[4096,1024]{1,0:T(8,128)(2,1)} custom-call(bf16[4096,1024]{1,0:T(8,128)(2,1)} %get-tuple-element.9.x_ref), custom_call_target="tpu_custom_call" | custom-call | bytes 16777216 | tf_op jit(solution)/shard_map/dup/pallas_call | solution.py:288
  203.0 0.0 copy-start.1
  203.0 9.0 %dup.4 = bf16[4096,1024]{1,0:T(8,128)(2,1)} custom-call(bf16[4096,1024]{1,0:T(8,128)(2,1)} %get-tuple-element.10.x_ref), custom_call_target="tpu_custom_call" | custom-call | bytes 16777216 | tf_op jit(solution)/shard_map/dup/pallas_call | solution.py:288
  211.9 0.0 copy-start.3
  211.9 9.0 %dup.5 = bf16[4096,1024]{1,0:T(8,128)(2,1)} custom-call(bf16[4096,1024]{1,0:T(8,128)(2,1)} %all-gather.2.cloned.1.call-done.x_ref), custom_call_target="tpu_custom_call" | custom-call | bytes 16777216 | tf_op jit(solution)/shard_map/dup/pallas_call | solution.py:288
  221.0 117.7 %reduce-scatter.2.cloned.1.call-done = bf16[1024,1024]{1,0:T(8,128)(2,1)} async-done(((bf16[1024,4096]{1,0:T(8,128)(2,1)}), bf16[1024,1024]{1,0:T(8,128)(2,1)}) %reduce-scatter.2.cloned.1.call-update) | async-done | bytes 2097168 | tf_op jit(solution)/shard_map/reduce_scatter | solution.py:338
  338.7 0.0 copy-done.3
  338.7 1.0 copy.25
  339.7 0.0 copy-done.1
  (2 shorter events, 0.0 us)
Async XLA Ops:
  7.2 115.9 %copy-start = (f32[16,256]{1,0:T(8,128)S(1)}, f32[16,256]{1,0:T(8,128)}, u32[]{:S(2)}) copy-start(f32[16,256]{1,0:T(8,128)} %param.12) | copy-start | bytes 49156
  7.2 13.7 %copy-start.4 = (f32[2,16,32,64]{3,2,1,0:T(8,128)S(1)}, f32[2,16,32,64]{3,2,1,0:T(8,128)}, u32[]{:S(2)}) copy-start(f32[2,16,32,64]{3,2,1,0:T(8,128)} %param.11) | copy-start | bytes 786436
  7.2 172.0 %all-gather.2.cloned.1.call-start = ((), (), s32[]{:S(2)}) async-start(), calls=%async_computation.1 | async-start | bytes 9437184 | tf_op jit(solution)/shard_map/all_gather | solution.py:330
  13.4 109.6 %copy-start.5 = (s32[16]{0:T(128)S(1)}, s32[16]{0:T(128)}, u32[]{:S(2)}) copy-start(s32[16]{0:T(128)} %param.13) | copy-start | bytes 196
  122.8 215.9 %reduce-scatter.2.cloned.1.call-start = ((), (), s32[]{:S(2)}) async-start(), calls=%async_computation.2 | async-start | bytes 10485760 | tf_op jit(solution)/shard_map/reduce_scatter | solution.py:338
  124.3 15.1 %copy-start.2 = (bf16[4096,1024]{1,0:T(8,128)(2,1)S(1)}, bf16[4096,1024]{1,0:T(8,128)(2,1)}, u32[]{:S(2)}) copy-start(bf16[4096,1024]{1,0:T(8,128)(2,1)} %get-tuple-element.9.x_ref) | copy-start | bytes 25165828
  203.0 136.7 %copy-start.1 = (f32[16,256]{1,0:T(8,128)S(1)}, f32[16,256]{1,0:T(8,128)}, u32[]{:S(2)}) copy-start(f32[16,256]{1,0:T(8,128)} %param.12) | copy-start | bytes 49156
  211.9 126.8 %copy-start.3 = (bf16[2,4,256,256]{3,2,1,0:T(8,128)(2,1)S(1)}, bf16[2,4,256,256]{3,2,1,0:T(8,128)(2,1)}, u32[]{:S(2)}) copy-start(bf16[2,4,256,256]{3,2,1,0:T(8,128)(2,1)} %get-tuple-element.22.g_ref) | copy-start | bytes 3145732
Sparse Core Ops, SparseCore 0:
  122.9 56.2 all-gather.1
  194.1 144.6 reduce-scatter.1

commit v4 on v3

--- a/solution.py
+++ b/solution.py
@@ -115,7 +115,7 @@
         return held.at[q // 2, z, :, :, pl.ds((q % 2) * half, half)]
 
     a2a, own = {}, {}
-    queue = [0, 1, 2, 6, 3, 4, 5]
+    queue = [0, 1, 2, 3, 6, 4, 5]
 
     def depart():
         q = queue.pop(0)
@@ -199,6 +199,10 @@
     first(1)
     relay(0)
     first(2)
+    relay(1)
+    first(3)
+    across(0)
+    relay(2)
     arrive(6)
     for h in range(2):
         for g in range(gpiece.shape[1]):
@@ -208,10 +212,6 @@
                 )
     first(4)
     first(5)
-    relay(1)
-    first(3)
-    across(0)
-    relay(2)
     relay(4)
     relay(5)
     assemble(4, piece2.at[pl.ds(0, half)])

time: 348 us -> 358 us (1.029)
  Pallas kernels: 144 us -> 156 us
    pallas_call x1, Pallas kernels: 101 us -> 113 us  [spread(): pl.pallas_call(spread_body, in_specs=[vmem] * 4, out_specs=[hbm, hbm, vme...]
  transfers between devices with their start and end apart: 2 -> 2, of which waited for: 2 -> 2; matrix products, arithmetic and copies ran while one was open for 8% -> 8% of each run, Pallas kernels for 13% -> 12%
where the time goes in v4:
time: 358 us; the launch traced here: 356 us
  Pallas kernels  156 us (44%)
  waiting for transfers between devices  126 us (35%)
  matrix products  42.3 us (12%)
  local copies, waits for them, and re-layouts  15.8 us (4%)
  between operations  14.1 us (4%)
    reduce_scatter x1, waiting for transfers between devices, on_device(): lax.psum_scatter(partial_value.astype(jnp.bfloat16), 'tensor', scatter_di...  118 us
    pallas_call x1, Pallas kernels, spread(): pl.pallas_call(spread_body, in_specs=[vmem] * 4, out_specs=[hbm, hbm, vme...  113 us
    pallas_call x3, Pallas kernels, dup(): pl.pallas_call(dup_body, grid=(rows // tile,), in_specs=[spec], out_specs...  27.1 us
    pallas_call x1, Pallas kernels, recur(): pl.pallas_call(functools.partial(recur_body, prompts), grid=(blocks, rows...  16.3 us
    dot_general x1, matrix products, on_device(): gate_pre = jnp.dot(tokens, branch_serve, preferred_element_type=jnp.float32)  15.2 us
    dot_general x1, matrix products, on_device(): lax.dot_general(gated, output_serve, (((1,), (1,)), ((), ())), preferred_...  14.7 us
    dot_general x1, matrix products, on_device(): jnp.dot(tokens, input_serve, preferred_element_type=jnp.float32)  12.4 us
    unnamed x16, local copies, waits for them, and re-layouts  9.13 us
  transfers between devices with their start and end apart: 2, of which 2 were waited for; matrix products, arithmetic and copies ran while one was open for 8% of the time, Pallas kernels for 12%

profile of v4, /device:TPU:0, one launch (start us, length us, event | category | flops | bytes accessed | tf_op | source)
XLA Modules:
  0.0 356.4 jit_solution(1230499527759714513)
XLA Ops:
  7.2 0.0 copy-start
  7.2 0.0 copy-start.4
  7.2 0.0 all-gather.2.cloned.1.call-start
  7.2 0.7 pad_clamp_fusion.1
  8.0 2.7 copy.22
  10.7 2.7 copy.21
  13.4 0.0 copy-start.5
  13.4 1.6 gather_fusion
  15.0 1.6 gather_fusion.1
  16.5 2.7 copy.20
  19.3 1.6 gather_fusion.2
  20.8 0.0 copy-done.4
  20.9 0.6 gather_fusion.3
  21.5 0.7 copy.23
  22.2 112.9 %spread.1 = (bf16[4096,1024]{1,0:T(8,128)(2,1)}, bf16[4096,1024]{1,0:T(8,128)(2,1)}, bf16[512,1024]{1,0:T(8,128)(2,1)}, bf16[2,4,256,256]{3,2,1,0:T(8,128)(2,1)}) custom-call(bf16[16,64,512]{2,1,0:T(8,128)(2,1)} %gather_fusion, bf16[16,64,512]{2,1,0:T(8,128)(2,1)} %gather_fusion.1, bf16[16,64,512]{2,1,0:T(8,128)(2,1)} %gather_fusion.2, ...), custom_call_target="tpu_custom_call" | custom-call | tf_op jit(solution)/shard_map/spread/pallas_call | solution.py:252
  135.2 0.0 all-gather.2.cloned.1.call-update
  135.2 0.2 reduce-scatter.2.cloned.1.call-start
  135.4 0.0 copy-done.5
  135.4 0.1 dynamic_slice.3
  135.5 0.0 copy-done
  135.5 0.6 gather_fusion.4
  136.1 0.6 fusion.r_ref
  136.7 0.0 copy-start.2
  136.7 15.2 %convolution_bitcast_fusion.pre_ref = f32[1024,1024]{1,0:T(8,128)} fusion(bf16[1024,4096]{1,0:T(8,128)(2,1)} %param.7, bf16[4096,1024]{1,0:T(8,128)(2,1)} %get-tuple-element.10.x_ref), kind=kOutput, calls=%fused_computation.6 | convolution fusion | flops 8589934592 | bytes 20971520 | tf_op jit(solution)/shard_map/dot_general | solution.py:333
  151.9 0.0 copy-done.2
  151.9 12.4 %convert_bitcast_fusion.x_ref = bf16[1024,1024]{1,0:T(8,128)(2,1)} fusion(bf16[1024,4096]{1,0:T(8,128)(2,1)} %param.7, bf16[4096,1024]{1,0:T(8,128)(2,1)S(1)} %copy-done.2), kind=kOutput, calls=%fused_computation.10 | convolution fusion | flops 8590983168 | bytes 18874368 | tf_op jit(solution)/shard_map/dot_general | solution.py:332
  164.3 16.3 %recur.1 = bf16[1024,1024]{1,0:T(8,128)(2,1)} custom-call(bf16[1024,1024]{1,0:T(8,128)(2,1)} %convert_bitcast_fusion.x_ref, f32[1024,1024]{1,0:T(8,128)} %convolution_bitcast_fusion.pre_ref, bf16[2,4,256,256]{3,2,1,0:T(8,128)(2,1)} %get-tuple-element.22.g_ref, f32[4,1,256]{2,1,0:T(1,128)} %fusion.r_ref), custom_call_target="tpu_custom_call" | custom-call | flops 1073741824 | bytes 8388608 | tf_op jit(solution)/shard_map/recur/pallas_call | solution.py:59
  180.6 8.4 %all-gather.2.cloned.1.call-done.x_ref = bf16[4096,1024]{1,0:T(8,128)(2,1)} async-done(((bf16[512,1024]{1,0:T(8,128)(2,1)}), bf16[4096,1024]{1,0:T(8,128)(2,1)}) %all-gather.2.cloned.1.call-update) | async-done | bytes 8388624 | tf_op jit(solution)/shard_map/all_gather | solution.py:330
  189.0 14.7 %convolution_convert_fusion = bf16[1024,4096]{1,0:T(8,128)(2,1)} fusion(bf16[1024,1024]{1,0:T(8,128)(2,1)} %recur.1, bf16[4096,1024]{1,0:T(8,128)(2,1)} %all-gather.2.cloned.1.call-done.x_ref), kind=kOutput, calls=%fused_computation.5 | convolution fusion | flops 8594128896 | bytes 18874368 | tf_op jit(solution)/shard_map/dot_general | solution.py:335
  203.8 0.0 reduce-scatter.2.cloned.1.call-update
  203.8 9.0 %dup.3 = bf16[4096,1024]{1,0:T(8,128)(2,1)} custom-call(bf16[4096,1024]{1,0:T(8,128)(2,1)} %get-tuple-element.9.x_ref), custom_call_target="tpu_custom_call" | custom-call | bytes 16777216 | tf_op jit(solution)/shard_map/dup/pallas_call | solution.py:288
  212.8 0.0 copy-start.1
  212.8 9.0 %dup.4 = bf16[4096,1024]{1,0:T(8,128)(2,1)} custom-call(bf16[4096,1024]{1,0:T(8,128)(2,1)} %get-tuple-element.10.x_ref), custom_call_target="tpu_custom_call" | custom-call | bytes 16777216 | tf_op jit(solution)/shard_map/dup/pallas_call | solution.py:288
  221.8 0.0 copy-start.3
  221.8 9.0 %dup.5 = bf16[4096,1024]{1,0:T(8,128)(2,1)} custom-call(bf16[4096,1024]{1,0:T(8,128)(2,1)} %all-gather.2.cloned.1.call-done.x_ref), custom_call_target="tpu_custom_call" | custom-call | bytes 16777216 | tf_op jit(solution)/shard_map/dup/pallas_call | solution.py:288
  230.8 117.7 %reduce-scatter.2.cloned.1.call-done = bf16[1024,1024]{1,0:T(8,128)(2,1)} async-done(((bf16[1024,4096]{1,0:T(8,128)(2,1)}), bf16[1024,1024]{1,0:T(8,128)(2,1)}) %reduce-scatter.2.cloned.1.call-update) | async-done | bytes 2097168 | tf_op jit(solution)/shard_map/reduce_scatter | solution.py:338
  348.5 0.0 copy-done.3
  348.5 1.0 copy.25
  349.5 0.0 copy-done.1
  (2 shorter events, 0.0 us)
Async XLA Ops:
  7.2 128.4 %copy-start = (f32[16,256]{1,0:T(8,128)S(1)}, f32[16,256]{1,0:T(8,128)}, u32[]{:S(2)}) copy-start(f32[16,256]{1,0:T(8,128)} %param.12) | copy-start | bytes 49156
  7.2 13.7 %copy-start.4 = (f32[2,16,32,64]{3,2,1,0:T(8,128)S(1)}, f32[2,16,32,64]{3,2,1,0:T(8,128)}, u32[]{:S(2)}) copy-start(f32[2,16,32,64]{3,2,1,0:T(8,128)} %param.11) | copy-start | bytes 786436
  7.2 181.8 %all-gather.2.cloned.1.call-start = ((), (), s32[]{:S(2)}) async-start(), calls=%async_computation.1 | async-start | bytes 9437184 | tf_op jit(solution)/shard_map/all_gather | solution.py:330
  13.4 122.1 %copy-start.5 = (s32[16]{0:T(128)S(1)}, s32[16]{0:T(128)}, u32[]{:S(2)}) copy-start(s32[16]{0:T(128)} %param.13) | copy-start | bytes 196
  135.2 213.4 %reduce-scatter.2.cloned.1.call-start = ((), (), s32[]{:S(2)}) async-start(), calls=%async_computation.2 | async-start | bytes 10485760 | tf_op jit(solution)/shard_map/reduce_scatter | solution.py:338
  136.7 15.2 %copy-start.2 = (bf16[4096,1024]{1,0:T(8,128)(2,1)S(1)}, bf16[4096,1024]{1,0:T(8,128)(2,1)}, u32[]{:S(2)}) copy-start(bf16[4096,1024]{1,0:T(8,128)(2,1)} %get-tuple-element.9.x_ref) | copy-start | bytes 25165828
  212.8 136.7 %copy-start.1 = (f32[16,256]{1,0:T(8,128)S(1)}, f32[16,256]{1,0:T(8,128)}, u32[]{:S(2)}) copy-start(f32[16,256]{1,0:T(8,128)} %param.12) | copy-start | bytes 49156
  221.8 126.8 %copy-start.3 = (bf16[2,4,256,256]{3,2,1,0:T(8,128)(2,1)S(1)}, bf16[2,4,256,256]{3,2,1,0:T(8,128)(2,1)}, u32[]{:S(2)}) copy-start(bf16[2,4,256,256]{3,2,1,0:T(8,128)(2,1)} %get-tuple-element.22.g_ref) | copy-start | bytes 3145732
Sparse Core Ops, SparseCore 0:
  135.3 53.6 all-gather.1
  203.9 144.6 reduce-scatter.1
